TPU v7x, 32 devices: a whole 2x2x4 slice. The times are simulated.
32 devices in a mesh: groups: 2 (over x), lon: 16 (over z, y, core).
Axes of the slice: x: 2, y: 2, z: 4, core: 2. Of those that a mesh axis runs over, the one named last changes fastest.
Arguments:
- input_field: bfloat16 [96, 512, 512], P('groups', 'lon'), parts along dimension 0, may hold values from -8 to 8
- expand_weight: bfloat16 [512, 2048], replicated, may hold values from -0.25 to 0.25
- expand_bias: float32 [2048], replicated, may hold values from -3 to 3
- depth_weight: float32 [9, 2048], replicated, may hold values from -2 to 2
- depth_bias: float32 [2048], replicated, may hold values from -3 to 3
- squeeze_down: bfloat16 [2048, 128], replicated, may hold values from -0.125 to 0.125
- squeeze_up: bfloat16 [128, 2048], replicated, may hold values from -3 to 3
- project_weight: bfloat16 [2048, 512], replicated, may hold values from -0.125 to 0.125
- block_gain: float32 [512], replicated, may hold values from 0.1 to 1.9
- block_in_weight: bfloat16 [512, 1536], replicated, may hold values from -4 to 4
- block_out_weight: bfloat16 [512, 512], replicated, may hold values from -0.25 to 0.25
- block_table: float32 [225, 16], replicated, may hold values from -5 to 5
- grid_gain: float32 [512], replicated, may hold values from 0.1 to 1.9
- grid_in_weight: bfloat16 [512, 1536], replicated, may hold values from -4 to 4
- grid_out_weight: bfloat16 [512, 512], replicated, may hold values from -0.25 to 0.25
- grid_table: float32 [225, 16], replicated, may hold values from -5 to 5
Outputs:
- output_field: bfloat16 [96, 512, 512], P('groups', 'lon'), parts along dimension 0
There are 2 independent parts, one for each index of `groups`. A program takes and returns all parts, laid end to end along the dimension named above; an argument that names none is the same for every part. Nothing has to cross between parts.
All inputs are finite; a program needn't handle non-finite values.
Results may differ from a plain program's by a relative error of at most 0.012.
Values may be sent and summed in bfloat16 or wider, within the bound.
No kernel may reach another device: no remote copies, remote signals or barrier semaphores. Data moves between devices by JAX's collectives and lax.ppermute only.
A program may use at most 128 MiB of HBM per device.

v0:
```python
import jax
import jax.numpy as jnp
from jax import lax
from jax.sharding import PartitionSpec as P

HEADS = 16
HEAD_DIM = 32


def extended(cells, sides, width):
    for axis, dim in sides:
        count = lax.axis_size(axis)
        head = lax.slice_in_dim(cells, 0, width, axis=dim)
        tail = lax.slice_in_dim(cells, cells.shape[dim] - width, cells.shape[dim], axis=dim)
        cells = jnp.concatenate(
            [
                lax.ppermute(tail, axis, [(i, (i + 1) % count) for i in range(count)]),
                cells,
                lax.ppermute(head, axis, [((i + 1) % count, i) for i in range(count)]),
            ],
            axis=dim,
        )
    return cells


def relative_bias(pos_table):
    position = jnp.arange(64)
    win_row = position // 8
    win_col = position % 8
    rel_index = (win_row[:, None] - win_row[None, :] + 7) * 15 + (
        win_col[:, None] - win_col[None, :] + 7
    )
    one_hot = (rel_index[:, :, None] == jnp.arange(225)[None, None, :]).astype(jnp.float32)
    return jnp.einsum("ijr,rh->hij", one_hot, pos_table, precision=lax.Precision.HIGHEST)


def layer_normed(stream, gain):
    widened = stream.astype(jnp.float32)
    average = jnp.mean(widened, axis=-1, keepdims=True)
    centred = widened - average
    variance = jnp.mean(centred * centred, axis=-1, keepdims=True)
    return (centred * lax.rsqrt(variance + 1e-05) * gain).astype(jnp.bfloat16)


def attend_windows(mixed, rel_bias):
    scores = jnp.einsum(
        "nqhd,nkhd->nhqk", mixed[:, :, 0], mixed[:, :, 1], preferred_element_type=jnp.float32
    )
    scores = scores * HEAD_DIM ** (-0.5) + rel_bias[None]
    scores = scores - jnp.max(scores, axis=-1, keepdims=True)
    exponent = jnp.exp(scores)
    probabilities = (exponent / jnp.sum(exponent, axis=-1, keepdims=True)).astype(jnp.bfloat16)
    return jnp.einsum(
        "nhqk,nkhd->nqhd", probabilities, mixed[:, :, 2], preferred_element_type=jnp.float32
    ).astype(jnp.bfloat16)


def expand_cells(cells, expand_weight, expand_bias):
    row_count, col_count, channels = cells.shape
    hidden = (
        jnp.dot(cells.reshape(-1, channels), expand_weight, preferred_element_type=jnp.float32)
        + expand_bias
    )
    return (
        jax.nn.gelu(hidden, approximate=False)
        .astype(jnp.bfloat16)
        .reshape(row_count, col_count, -1)
    )


def mbconv_block(
    input_field,
    expand_weight,
    expand_bias,
    depth_weight,
    depth_bias,
    squeeze_down,
    squeeze_up,
    project_weight,
):
    row_count, col_count, channels = input_field.shape
    hidden = expand_cells(input_field, expand_weight, expand_bias)
    rimmed = extended(hidden, (("lon", 1),), 1)
    padded = jnp.pad(rimmed, ((1, 1), (0, 0), (0, 0)))
    summed = depth_bias + jnp.zeros((row_count, col_count, depth_bias.shape[0]), jnp.float32)
    for row_off in range(3):
        for col_off in range(3):
            summed = (
                summed
                + padded[row_off : row_off + row_count, col_off : col_off + col_count].astype(
                    jnp.float32
                )
                * depth_weight[row_off * 3 + col_off]
            )
    active = jax.nn.gelu(summed, approximate=False).astype(jnp.bfloat16)
    partial_sum = jnp.sum(active, axis=(0, 1), dtype=jnp.float32)
    pooled = lax.psum(partial_sum, "lon") / (row_count * col_count * lax.axis_size("lon"))
    squeezed = jax.nn.silu(
        jnp.dot(pooled, squeeze_down.astype(jnp.float32), precision=lax.Precision.HIGHEST)
    )
    gate_value = jax.nn.sigmoid(
        jnp.dot(squeezed, squeeze_up.astype(jnp.float32), precision=lax.Precision.HIGHEST)
    )
    gated_act = (active * gate_value).astype(jnp.bfloat16)
    result = jnp.dot(
        gated_act.reshape(-1, gated_act.shape[-1]),
        project_weight,
        preferred_element_type=jnp.float32,
    )
    result = result + input_field.reshape(-1, channels).astype(jnp.float32)
    return result.astype(jnp.bfloat16).reshape(row_count, col_count, channels)


def block_attention(stream, gain, in_weight, out_weight, pos_table):
    row_count, col_count, channels = stream.shape
    normed = layer_normed(stream, gain)
    mixed = jnp.dot(
        normed.reshape(-1, channels), in_weight, preferred_element_type=jnp.float32
    ).astype(jnp.bfloat16)
    mixed = mixed.reshape(row_count // 8, 8, col_count // 8, 8, 3 * channels).transpose(
        0, 2, 1, 3, 4
    )
    mixed = mixed.reshape(-1, 64, 3, HEADS, HEAD_DIM)
    heads_out = attend_windows(mixed, relative_bias(pos_table))
    heads_out = (
        heads_out.reshape(row_count // 8, col_count // 8, 8, 8, channels)
        .transpose(0, 2, 1, 3, 4)
        .reshape(-1, channels)
    )
    merged = jnp.dot(heads_out, out_weight, preferred_element_type=jnp.float32) + stream.reshape(
        -1, channels
    ).astype(jnp.float32)
    return merged.astype(jnp.bfloat16).reshape(row_count, col_count, channels)


def grid_windows(tensor):
    row_count, items, lon_count, channels = tensor.shape
    shaped = tensor.reshape(8, row_count // 8, items, 8, lon_count // 8, channels)
    return shaped.transpose(1, 2, 4, 0, 3, 5).reshape(-1, 64, channels)


def grid_restore(windows, row_count, items, lon_count):
    channels = windows.shape[-1]
    shaped = windows.reshape(row_count // 8, items, lon_count // 8, 8, 8, channels)
    return shaped.transpose(3, 0, 1, 4, 2, 5).reshape(row_count, items, lon_count, channels)


def grid_attend(mixed, rel_bias):
    row_count, items, lon_count, triple_width = mixed.shape
    windows = grid_windows(mixed).reshape(-1, 64, 3, HEADS, HEAD_DIM)
    heads_out = attend_windows(windows, rel_bias).reshape(-1, 64, triple_width // 3)
    return grid_restore(heads_out, row_count, items, lon_count)


def grid_attention(stream, gain, in_weight, out_weight, pos_table):
    row_count, col_count, channels = stream.shape
    lon_count = lax.axis_size("lon")
    items = col_count // lon_count
    rel_bias = relative_bias(pos_table)
    normed = layer_normed(stream, gain)
    mixed = jnp.dot(
        normed.reshape(-1, channels), in_weight, preferred_element_type=jnp.float32
    ).astype(jnp.bfloat16)
    mixed = mixed.reshape(row_count, items, lon_count, 3 * channels)
    heads_out = grid_attend(
        lax.all_to_all(mixed, "lon", split_axis=2, concat_axis=2, tiled=True), rel_bias
    )
    returned = lax.all_to_all(heads_out, "lon", split_axis=2, concat_axis=2, tiled=True)
    merged = jnp.dot(returned.reshape(-1, channels), out_weight, preferred_element_type=jnp.float32)
    merged = merged + stream.reshape(-1, channels).astype(jnp.float32)
    return merged.astype(jnp.bfloat16).reshape(row_count, col_count, channels)


def per_device(
    input_field,
    expand_weight,
    expand_bias,
    depth_weight,
    depth_bias,
    squeeze_down,
    squeeze_up,
    project_weight,
    block_gain,
    block_in_weight,
    block_out_weight,
    block_table,
    grid_gain,
    grid_in_weight,
    grid_out_weight,
    grid_table,
):
    first_stream = mbconv_block(
        input_field,
        expand_weight,
        expand_bias,
        depth_weight,
        depth_bias,
        squeeze_down,
        squeeze_up,
        project_weight,
    )
    second_stream = block_attention(
        first_stream, block_gain, block_in_weight, block_out_weight, block_table
    )
    return grid_attention(second_stream, grid_gain, grid_in_weight, grid_out_weight, grid_table)


def solution(mesh):
    return jax.shard_map(
        per_device,
        mesh=mesh,
        in_specs=(
            P("groups", "lon", None),
            P(),
            P(),
            P(),
            P(),
            P(),
            P(),
            P(),
            P(),
            P(),
            P(),
            P(),
            P(),
            P(),
            P(),
            P(),
        ),
        out_specs=P("groups", "lon", None),
        check_vma=False,
    )
```

profile of v0, /device:TPU:1, one launch (start us, length us, event | category | flops | bytes accessed | tf_op | source)
XLA Modules:
  0.0 534.6 jit_solution(4356687229449048533)
XLA Ops:
  1.6 30.8 %fusion.6 = bf16[1536,2048]{1,0:T(8,128)(2,1)S(1)} fusion(bf16[1536,512]{1,0:T(8,128)(2,1)} %bitcast.114, bf16[512,2048]{1,0:T(8,128)(2,1)S(1)} %copy-done, f32[2048]{0:T(1024)} %param.18), kind=kOutput, calls=%fused_computation.12 | convolution fusion | flops 3428843520 | bytes 9969664 | tf_op jit(solution)/shard_map/dot_general | solution.py:61
  56.3 48.9 %convert_reduce_fusion = (f32[2048]{0:T(1024)S(1)}, bf16[48,32,2048]{2,1,0:T(8,128)(2,1)}) fusion(f32[2048]{0:T(1024)S(1)} %bitcast.110, bf16[50,34,2048]{2,1,0:T(8,128)(2,1)S(1)} %fusion.30, f32[2048]{0:T(1024)S(1)} %bitcast.111, f32[2048]{0:T(1024)S(1)} %bitcast.104, f32[2048]{0:T(1024)S(1)} %bitcast.105, ...), kind=kLoop, calls=%fused_computation.8 | loop fusion | flops 314570752 | bytes 50814976 | tf_op jit(solution)/shard_map/reduce_sum | solution.py:96
  105.2 28.6 %psum.7 = f32[2048]{0:T(1024)S(1)} all-reduce(f32[2048]{0:T(1024)S(1)} %get-tuple-element.5), channel_id=1, replica_groups=mesh['groups'=2,'lon'=16] {'lon'}, use_global_device_ids=true, to_apply=%region_1.2 | all-reduce | flops 2048 | bytes 16384 | tf_op jit(solution)/shard_map/psum | solution.py:97
  150.9 21.1 %reshape.215 = bf16[24,64,3,16,32]{4,3,2,1,0:T(8,128)(2,1)} reshape(bf16[6,4,8,8,1536]{4,3,2,1,0:T(8,128)(2,1)} %bitcast.94) | data formatting | bytes 9437184 | tf_op jit(solution)/shard_map/reshape | solution.py:123
  172.0 14.3 %fusion.88 = (bf16[24,64,1,16,32]{4,3,2,1,0:T(8,128)(2,1)}, bf16[24,64,1,16,32]{4,3,2,1,0:T(8,128)(2,1)}, bf16[24,64,1,16,32]{4,3,2,1,0:T(8,128)(2,1)}) fusion(bf16[24,64,3,16,32]{4,3,2,1,0:T(8,128)(2,1)} %reshape.215), kind=kLoop, calls=%fused_computation.139 | loop fusion | bytes 9437184 | tf_op jit(solution)/shard_map/slice | solution.py:54
  186.4 8.0 %copy.79 = bf16[24,64,1,16,32]{1,4,3,0,2:T(8,128)(2,1)} copy(bf16[24,64,1,16,32]{4,3,2,1,0:T(8,128)(2,1)} %get-tuple-element.11) | data formatting | bytes 3145728
  194.4 8.0 %copy.80 = bf16[24,64,1,16,32]{1,4,3,0,2:T(8,128)(2,1)} copy(bf16[24,64,1,16,32]{4,3,2,1,0:T(8,128)(2,1)} %get-tuple-element.12) | data formatting | bytes 3145728
  202.4 8.0 %copy.78 = bf16[24,64,1,16,32]{1,4,3,0,2:T(8,128)(2,1)} copy(bf16[24,64,1,16,32]{4,3,2,1,0:T(8,128)(2,1)} %get-tuple-element.10) | data formatting | bytes 3145728
  215.1 8.3 %fusion.91 = (f32[24,16,64]{2,1,0:T(8,128)S(1)}, f32[24,16,64,64]{2,3,1,0:T(8,128)}) fusion(f32[24,16,64,64]{2,3,1,0:T(8,128)S(1)} %fusion.53, f32[16,64,64]{1,2,0:T(8,128)S(1)} %copy.58), kind=kOutput, calls=%fused_computation.142 | output fusion | flops 9437247 | bytes 12943360 | tf_op jit(solution)/shard_map/sub | solution.py:50
  223.4 9.0 %convert_bitcast_fusion.1 = bf16[24,64,16,32]{1,3,2,0:T(8,128)(2,1)} fusion(f32[24,16,64,64]{2,3,1,0:T(8,128)} %get-tuple-element.27, f32[24,16,64]{2,1,0:T(8,128)S(1)} %get-tuple-element.26, bf16[24,64,1,16,32]{1,4,3,0,2:T(8,128)(2,1)} %copy.78), kind=kOutput, calls=%fused_computation.100 | convolution fusion | flops 104595456 | bytes 9535488 | tf_op jit(solution)/shard_map/nhqk,nkhd->nqhd/dot_general | solution.py:53
  232.4 7.9 %copy.60 = bf16[24,64,16,32]{3,2,1,0:T(8,128)(2,1)} copy(bf16[24,64,16,32]{1,3,2,0:T(8,128)(2,1)} %convert_bitcast_fusion.1) | data formatting | bytes 3145728 | tf_op jit(solution)/shard_map/convert_element_type | solution.py:55
  240.3 8.4 %reshape.216 = bf16[6,4,8,8,512]{4,3,2,1,0:T(8,128)(2,1)S(1)} reshape(bf16[24,64,16,32]{3,2,1,0:T(8,128)(2,1)} %copy.60) | data formatting | bytes 3145728 | tf_op jit(solution)/shard_map/reshape | solution.py:126
  258.3 9.4 %copy.62 = bf16[48,2,16,1536]{3,1,0,2:T(2,128)(2,1)} copy(bf16[48,2,16,1536]{3,2,1,0:T(8,128)(2,1)} %bitcast.100) | data formatting | bytes 9437184 | tf_op jit(solution)/shard_map/reshape | solution.py:164
  279.1 83.6 %all-to-all-done = bf16[48,2,16,1536]{3,1,0,2:T(2,128)(2,1)} async-done(((bf16[48,2,16,1536]{3,1,0,2:T(2,128)(2,1)}), bf16[48,2,16,1536]{3,1,0,2:T(2,128)(2,1)}, u32[]{:S(2)}, u32[]{:S(2)}) %all-to-all-start) | async-done | bytes 4718624 | tf_op jit(solution)/shard_map/all_to_all | solution.py:166
  369.8 21.1 %reshape_reshape.6 = bf16[24,64,3,16,32]{4,3,2,1,0:T(8,128)(2,1)} reshape(bf16[6,2,2,8,8,1536]{5,4,3,2,1,0:T(8,128)(2,1)} %copy.64) | data formatting | bytes 9437184 | tf_op jit(solution)/shard_map/reshape;reshape | solution.py:150
  390.9 14.3 %fusion.87 = (bf16[24,64,1,16,32]{4,3,2,1,0:T(8,128)(2,1)}, bf16[24,64,1,16,32]{4,3,2,1,0:T(8,128)(2,1)}, bf16[24,64,1,16,32]{4,3,2,1,0:T(8,128)(2,1)}) fusion(bf16[24,64,3,16,32]{4,3,2,1,0:T(8,128)(2,1)} %reshape_reshape.6), kind=kLoop, calls=%fused_computation.138 | loop fusion | bytes 9437184 | tf_op jit(solution)/shard_map/slice | solution.py:54
  405.3 8.0 %copy.82 = bf16[24,64,1,16,32]{1,4,3,0,2:T(8,128)(2,1)} copy(bf16[24,64,1,16,32]{4,3,2,1,0:T(8,128)(2,1)} %get-tuple-element.8) | data formatting | bytes 3145728
  413.3 8.0 %copy.83 = bf16[24,64,1,16,32]{1,4,3,0,2:T(8,128)(2,1)} copy(bf16[24,64,1,16,32]{4,3,2,1,0:T(8,128)(2,1)} %get-tuple-element.9) | data formatting | bytes 3145728
  421.3 8.0 %copy.81 = bf16[24,64,1,16,32]{1,4,3,0,2:T(8,128)(2,1)} copy(bf16[24,64,1,16,32]{4,3,2,1,0:T(8,128)(2,1)} %get-tuple-element.7) | data formatting | bytes 3145728
  434.0 8.2 %fusion.92 = (f32[24,16,64]{2,1,0:T(8,128)S(1)}, f32[24,16,64,64]{2,3,1,0:T(8,128)}) fusion(f32[24,16,64,64]{2,3,1,0:T(8,128)S(1)} %fusion.49, f32[16,64,64]{1,2,0:T(8,128)S(1)} %copy.68), kind=kOutput, calls=%fused_computation.143 | output fusion | flops 9437247 | bytes 12943360 | tf_op jit(solution)/shard_map/sub | solution.py:50
  442.3 9.0 %convert_bitcast_fusion = bf16[24,64,16,32]{1,3,2,0:T(8,128)(2,1)} fusion(f32[24,16,64,64]{2,3,1,0:T(8,128)} %get-tuple-element.31, f32[24,16,64]{2,1,0:T(8,128)S(1)} %get-tuple-element.30, bf16[24,64,1,16,32]{1,4,3,0,2:T(8,128)(2,1)} %copy.81), kind=kOutput, calls=%fused_computation.99 | convolution fusion | flops 104595456 | bytes 9535488 | tf_op jit(solution)/shard_map/nhqk,nkhd->nqhd/dot_general | solution.py:53
  451.2 8.0 %copy.70 = bf16[24,64,16,32]{3,2,1,0:T(8,128)(2,1)} copy(bf16[24,64,16,32]{1,3,2,0:T(8,128)(2,1)} %convert_bitcast_fusion) | data formatting | bytes 3145728 | tf_op jit(solution)/shard_map/convert_element_type | solution.py:55
  459.3 9.3 %reshape_reshape.7 = bf16[6,2,2,8,8,512]{5,4,3,2,1,0:T(8,128)(2,1)} reshape(bf16[24,64,16,32]{3,2,1,0:T(8,128)(2,1)} %copy.70) | data formatting | bytes 3145728 | tf_op jit(solution)/shard_map/reshape;reshape | solution.py:144
  471.6 57.6 %all_to_all.10 = bf16[48,2,16,512]{3,1,0,2:T(2,128)(2,1)S(1)} all-to-all(bf16[48,2,16,512]{3,1,0,2:T(2,128)(2,1)S(1)} %bitcast.95), channel_id=1, replica_groups=mesh['groups'=2,'lon'=16] {'lon'}, dimensions={2} | all-to-all | bytes 3145728 | tf_op jit(solution)/shard_map/all_to_all | solution.py:168
  (71 shorter events, 88.1 us)
Async XLA Ops:
  0.0 1.6 copy-start
  1.6 36.8 %copy-start.7 = (f32[9,2048]{1,0:T(8,128)S(1)}, f32[9,2048]{1,0:T(8,128)}, u32[]{:S(2)}) copy-start(f32[9,2048]{1,0:T(8,128)} %param.19) | copy-start | bytes 221188
  1.6 37.0 %copy-start.13 = (f32[225,16]{0,1:T(8,128)S(1)}, f32[225,16]{0,1:T(8,128)}, u32[]{:S(2)}) copy-start(f32[225,16]{0,1:T(8,128)} %param.27) | copy-start | bytes 43204
  32.4 2.7 copy-start.2
  32.4 23.9 %copy-start.8 = (f32[2048]{0:T(1024)S(1)}, f32[2048]{0:T(1024)}, u32[]{:S(2)}) copy-start(f32[2048]{0:T(1024)} %param.20) | copy-start | bytes 24580
  35.7 11.6 %collective-permute-start = (bf16[48,1,2048]{2,1,0:T(2,128)(2,1)S(1)}, bf16[48,1,2048]{2,1,0:T(2,128)(2,1)S(1)}, u32[]{:S(2)}, u32[]{:S(2)}) collective-permute-start(bf16[48,1,2048]{2,1,0:T(2,128)(2,1)S(1)} %get-tuple-element.13), channel_id=1, source_target_pairs={{0,1},{1,2},{2,3},{3,4},{4,5},{5,6},{6,7},{7,8},{8,9},{9,10},{10,1... | collective-permute-start | bytes 589832 | tf_op jit(solution)/shard_map/ppermute | solution.py:17
  38.4 11.4 %collective-permute-start.1 = (bf16[48,1,2048]{2,1,0:T(2,128)(2,1)S(1)}, bf16[48,1,2048]{2,1,0:T(2,128)(2,1)S(1)}, u32[]{:S(2)}, u32[]{:S(2)}) collective-permute-start(bf16[48,1,2048]{2,1,0:T(2,128)(2,1)S(1)} %get-tuple-element.14), channel_id=1, source_target_pairs={{1,0},{2,1},{3,2},{4,3},{5,4},{6,5},{7,6},{8,7},{9,8},{10,9},{11,1... | collective-permute-start | bytes 589832 | tf_op jit(solution)/shard_map/ppermute | solution.py:19
  56.3 77.5 %copy-start.5 = (bf16[2048,128]{1,0:T(8,128)(2,1)S(1)}, bf16[2048,128]{1,0:T(8,128)(2,1)}, u32[]{:S(2)}) copy-start(bf16[2048,128]{1,0:T(8,128)(2,1)} %param.21) | copy-start | bytes 1572868
  56.3 77.8 %copy-start.6 = (bf16[128,2048]{1,0:T(8,128)(2,1)S(1)}, bf16[128,2048]{1,0:T(8,128)(2,1)}, u32[]{:S(2)}) copy-start(bf16[128,2048]{1,0:T(8,128)(2,1)} %param.22) | copy-start | bytes 1572868
  133.8 5.3 copy-start.9
  139.1 5.9 %copy-start.10 = (bf16[512,1536]{1,0:T(8,128)(2,1)S(1)}, bf16[512,1536]{1,0:T(8,128)(2,1)}, u32[]{:S(2)}) copy-start(bf16[512,1536]{1,0:T(8,128)(2,1)} %param.25) | copy-start | bytes 4718596
  139.1 5.9 %copy-start.15 = (f32[512]{0:T(512)S(1)}, f32[512]{0:T(512)}, u32[]{:S(2)}) copy-start(f32[512]{0:T(512)} %param.24) | copy-start | bytes 6148
  144.1 6.8 %copy-start.4 = (bf16[1536,512]{1,0:T(8,128)(2,1)}, bf16[1536,512]{1,0:T(8,128)(2,1)S(1)}, u32[]{:S(2)}) copy-start(bf16[1536,512]{1,0:T(8,128)(2,1)S(1)} %get-tuple-element.25) | copy-start | bytes 4718596
  232.4 16.5 %copy-start.11 = (bf16[512,512]{1,0:T(8,128)(2,1)S(1)}, bf16[512,512]{1,0:T(8,128)(2,1)}, u32[]{:S(2)}) copy-start(bf16[512,512]{1,0:T(8,128)(2,1)} %param.26) | copy-start | bytes 1572868
  232.4 19.9 %copy-start.16 = (f32[512]{0:T(512)S(1)}, f32[512]{0:T(512)}, u32[]{:S(2)}) copy-start(f32[512]{0:T(512)} %param.28) | copy-start | bytes 6148
  251.4 16.3 %copy-start.3 = (bf16[1536,512]{1,0:T(8,128)(2,1)}, bf16[1536,512]{1,0:T(8,128)(2,1)S(1)}, u32[]{:S(2)}) copy-start(bf16[1536,512]{1,0:T(8,128)(2,1)S(1)} %get-tuple-element.29) | copy-start | bytes 4718596
  258.3 17.3 %copy-start.14 = (f32[225,16]{0,1:T(8,128)S(1)}, f32[225,16]{0,1:T(8,128)}, u32[]{:S(2)}) copy-start(f32[225,16]{0,1:T(8,128)} %param.31) | copy-start | bytes 43204
  267.7 95.0 %all-to-all-start = ((bf16[48,2,16,1536]{3,1,0,2:T(2,128)(2,1)}), bf16[48,2,16,1536]{3,1,0,2:T(2,128)(2,1)}, u32[]{:S(2)}, u32[]{:S(2)}) async-start(bf16[48,2,16,1536]{3,1,0,2:T(2,128)(2,1)} %copy.62), calls=%async_computation | async-start | bytes 9437184 | tf_op jit(solution)/shard_map/all_to_all | solution.py:166
  451.2 79.6 %copy-start.12 = (bf16[512,512]{1,0:T(8,128)(2,1)S(1)}, bf16[512,512]{1,0:T(8,128)(2,1)}, u32[]{:S(2)}) copy-start(bf16[512,512]{1,0:T(8,128)(2,1)} %param.30) | copy-start | bytes 1572868
  451.2 83.2 %copy-start.1 = (bf16[512,2048]{1,0:T(8,128)(2,1)S(1)}, bf16[512,2048]{1,0:T(8,128)(2,1)}, u32[]{:S(2)}) copy-start(bf16[512,2048]{1,0:T(8,128)(2,1)} %param.17) | copy-start | bytes 6291460
where the time goes:
time: 544 us; the launch traced here: 535 us
  local copies, waits for them, and re-layouts  182 us (33%)
  waiting for transfers between devices  91.4 us (17%)
  blocking collectives  86.2 us (16%)
  matrix products  85.6 us (16%)
  other arithmetic  78.1 us (14%)
  starting transfers between devices  10.6 us (2%)
    all_to_all x1, waiting for transfers between devices, grid_attention(): lax.all_to_all(mixed, 'lon', split_axis=2, concat_axis=2, tiled=True)  83.6 us
    all_to_all x1, blocking collectives, grid_attention(): lax.all_to_all(heads_out, 'lon', split_axis=2, concat_axis=2, tiled=True)  57.6 us
    unnamed x40, local copies, waits for them, and re-layouts  52.4 us
    reduce_sum x1, other arithmetic, mbconv_block(): partial_sum = jnp.sum(active, axis=(0, 1), dtype=jnp.float32)  48.9 us
    dot_general x1, matrix products, expand_cells(): jnp.dot(cells.reshape(-1, channels), expand_weight, preferred_element_typ...  30.8 us
    slice x2, local copies, waits for them, and re-layouts, attend_windows(): mixed[:, :, 2]  28.7 us
    psum x1, blocking collectives, mbconv_block(): lax.psum(partial_sum, 'lon')  28.6 us
    reshape x1, local copies, waits for them, and re-layouts, block_attention(): mixed = mixed.reshape(-1, 64, 3, HEADS, HEAD_DIM)  21.1 us
  transfers between devices with their start and end apart: 3, of which 3 were waited for; matrix products, arithmetic and copies ran while one was open for 1% of the time, Pallas kernels for 0%

commit v1 on v0

--- a/solution.py
+++ b/solution.py
@@ -5,6 +5,21 @@
 
 HEADS = 16
 HEAD_DIM = 32
+
+
+def put_the_local_data(mine, along_dim, v0):
+    y1 = mine.shape
+    return jnp.moveaxis(
+        mine.reshape(*y1[:along_dim], v0, y1[along_dim] // v0, *y1[along_dim + 1 :]), along_dim, 0
+    )
+
+
+def balance_the_cells(frame, d_out):
+    frame = jnp.moveaxis(frame, 0, d_out)
+    block_last = frame.shape
+    return frame.reshape(
+        *block_last[:d_out], block_last[d_out] * block_last[d_out + 1], *block_last[d_out + 2 :]
+    )
 
 
 def extended(cells, sides, width):
@@ -153,6 +168,19 @@
 
 
 def grid_attention(stream, gain, in_weight, out_weight, pos_table):
+
+    def _unite_surface(unit, dev_axis, array_here, q_in):
+        fresh, side_arr = (jax.lax.axis_size(dev_axis), jax.lax.axis_index(dev_axis))
+        all_rows = put_the_local_data(unit, array_here, fresh)
+        shelf = [all_rows[side_arr]]
+        for src_i in range(1, fresh):
+            finding = all_rows[side_arr ^ src_i]
+            shelf.append(
+                jax.lax.ppermute(finding, dev_axis, [(j0, j0 ^ src_i) for j0 in range(fresh)])
+            )
+        all_rows = jnp.stack(shelf)[side_arr ^ jnp.arange(fresh)]
+        return balance_the_cells(all_rows, q_in)
+
     row_count, col_count, channels = stream.shape
     lon_count = lax.axis_size("lon")
     items = col_count // lon_count
@@ -162,9 +190,7 @@
         normed.reshape(-1, channels), in_weight, preferred_element_type=jnp.float32
     ).astype(jnp.bfloat16)
     mixed = mixed.reshape(row_count, items, lon_count, 3 * channels)
-    heads_out = grid_attend(
-        lax.all_to_all(mixed, "lon", split_axis=2, concat_axis=2, tiled=True), rel_bias
-    )
+    heads_out = grid_attend(_unite_surface(mixed, "lon", 2, 2), rel_bias)
     returned = lax.all_to_all(heads_out, "lon", split_axis=2, concat_axis=2, tiled=True)
     merged = jnp.dot(returned.reshape(-1, channels), out_weight, preferred_element_type=jnp.float32)
     merged = merged + stream.reshape(-1, channels).astype(jnp.float32)

time: 544 us -> 572 us (1.051)
  local copies, waits for them, and re-layouts: 182 us -> 214 us
  waiting for transfers between devices: 91.4 us -> 74.4 us
  starting transfers between devices: 10.6 us -> 20 us
    all_to_all x1 -> x0, waiting for transfers between devices: 83.6 us -> none  [grid_attention(): lax.all_to_all(mixed, 'lon', split_axis=2, concat_axis=2, tiled=True)]
    ppermute x0 -> x15, waiting for transfers between devices: none -> 70.9 us  [_unite_surface(): jax.lax.ppermute(finding, dev_axis, [(j0, j0 ^ src_i) for j0 in range(fre...]
    ppermute x0 -> x15, starting transfers between devices: none -> 17.3 us  [_unite_surface(): jax.lax.ppermute(finding, dev_axis, [(j0, j0 ^ src_i) for j0 in range(fre...]
    another operation x0 -> x2, local copies, waits for them, and re-layouts: none -> 14 us
    unnamed x40 -> x72, local copies, waits for them, and re-layouts: 52.4 us -> 65.3 us
    transpose x0 -> x1, local copies, waits for them, and re-layouts: none -> 9.37 us  [balance_the_cells(): frame = jnp.moveaxis(frame, 0, d_out)]
    reshape x1 -> x0, local copies, waits for them, and re-layouts: 9.36 us -> none  [grid_attention(): mixed = mixed.reshape(row_count, items, lon_count, 3 * channels)]
    all_to_all x1 -> x0, starting transfers between devices: 7.92 us -> none  [grid_attention(): lax.all_to_all(mixed, 'lon', split_axis=2, concat_axis=2, tiled=True)]
  transfers between devices with their start and end apart: 3 -> 17, of which waited for: 3 -> 9; matrix products, arithmetic and copies ran while one was open for 1% -> 4% of each run, Pallas kernels for 0% -> 0%
where the time goes in v1:
time: 572 us; the launch traced here: 562 us
  local copies, waits for them, and re-layouts  214 us (37%)
  blocking collectives  90.2 us (16%)
  matrix products  84.2 us (15%)
  other arithmetic  78.2 us (14%)
  waiting for transfers between devices  74.4 us (13%)
  starting transfers between devices  20 us (3%)
    ppermute x15, waiting for transfers between devices, _unite_surface(): jax.lax.ppermute(finding, dev_axis, [(j0, j0 ^ src_i) for j0 in range(fre...  70.9 us
    unnamed x72, local copies, waits for them, and re-layouts  65.3 us
    all_to_all x1, blocking collectives, grid_attention(): lax.all_to_all(heads_out, 'lon', split_axis=2, concat_axis=2, tiled=True)  61.2 us
    reduce_sum x1, other arithmetic, mbconv_block(): partial_sum = jnp.sum(active, axis=(0, 1), dtype=jnp.float32)  48.9 us
    dot_general x1, matrix products, expand_cells(): jnp.dot(cells.reshape(-1, channels), expand_weight, preferred_element_typ...  30.8 us
    psum x1, blocking collectives, mbconv_block(): lax.psum(partial_sum, 'lon')  29 us
    slice x2, local copies, waits for them, and re-layouts, attend_windows(): mixed[:, :, 2]  28.5 us
    reshape x1, local copies, waits for them, and re-layouts, block_attention(): mixed = mixed.reshape(-1, 64, 3, HEADS, HEAD_DIM)  21.1 us
  transfers between devices with their start and end apart: 17, of which 9 were waited for; matrix products, arithmetic and copies ran while one was open for 4% of the time, Pallas kernels for 0%

profile of v1, /device:TPU:1, one launch (start us, length us, event | category | flops | bytes accessed | tf_op | source)
XLA Modules:
  0.0 561.8 jit_solution(14116750661190454981)
XLA Ops:
  1.6 30.8 %fusion.6 = bf16[1536,2048]{1,0:T(8,128)(2,1)S(1)} fusion(bf16[1536,512]{1,0:T(8,128)(2,1)} %bitcast.246, bf16[512,2048]{1,0:T(8,128)(2,1)S(1)} %copy-done, f32[2048]{0:T(1024)} %param.18), kind=kOutput, calls=%fused_computation.13 | convolution fusion | flops 3428843520 | bytes 9969664 | tf_op jit(solution)/shard_map/dot_general | solution.py:76
  56.3 48.9 %convert_reduce_fusion = (f32[2048]{0:T(1024)S(1)}, bf16[48,32,2048]{2,1,0:T(8,128)(2,1)}) fusion(f32[2048]{0:T(1024)S(1)} %bitcast.242, bf16[50,34,2048]{2,1,0:T(8,128)(2,1)S(1)} %fusion.30, f32[2048]{0:T(1024)S(1)} %bitcast.243, f32[2048]{0:T(1024)S(1)} %bitcast.236, f32[2048]{0:T(1024)S(1)} %bitcast.237, ...), kind=kLoop, calls=%fused_computation.9 | loop fusion | flops 314570752 | bytes 50814976 | tf_op jit(solution)/shard_map/reduce_sum | solution.py:111
  105.2 29.0 %psum.7 = f32[2048]{0:T(1024)S(1)} all-reduce(f32[2048]{0:T(1024)S(1)} %get-tuple-element.5), channel_id=1, replica_groups=mesh['groups'=2,'lon'=16] {'lon'}, use_global_device_ids=true, to_apply=%region_1.2 | all-reduce | flops 2048 | bytes 16384 | tf_op jit(solution)/shard_map/psum | solution.py:112
  151.4 21.1 %reshape.256 = bf16[24,64,3,16,32]{4,3,2,1,0:T(8,128)(2,1)} reshape(bf16[6,4,8,8,1536]{4,3,2,1,0:T(8,128)(2,1)} %bitcast.212) | data formatting | bytes 9437184 | tf_op jit(solution)/shard_map/reshape | solution.py:138
  172.6 14.3 %fusion.90 = (bf16[24,64,1,16,32]{4,3,2,1,0:T(8,128)(2,1)}, bf16[24,64,1,16,32]{4,3,2,1,0:T(8,128)(2,1)}, bf16[24,64,1,16,32]{4,3,2,1,0:T(8,128)(2,1)}) fusion(bf16[24,64,3,16,32]{4,3,2,1,0:T(8,128)(2,1)} %reshape.256), kind=kLoop, calls=%fused_computation.191 | loop fusion | bytes 9437184 | tf_op jit(solution)/shard_map/slice | solution.py:69
  194.8 8.0 %copy.172 = bf16[24,64,1,16,32]{1,4,3,0,2:T(8,128)(2,1)} copy(bf16[24,64,1,16,32]{4,3,2,1,0:T(8,128)(2,1)} %get-tuple-element.12) | data formatting | bytes 3145728
  202.9 8.0 %copy.170 = bf16[24,64,1,16,32]{1,4,3,0,2:T(8,128)(2,1)} copy(bf16[24,64,1,16,32]{4,3,2,1,0:T(8,128)(2,1)} %get-tuple-element.10) | data formatting | bytes 3145728
  215.6 8.5 %fusion.93 = (f32[24,16,64]{2,1,0:T(8,128)S(1)}, f32[24,16,64,64]{2,3,1,0:T(8,128)}) fusion(f32[24,16,64,64]{2,3,1,0:T(8,128)S(1)} %fusion.53, f32[16,64,64]{1,2,0:T(8,128)S(1)} %copy.121), kind=kOutput, calls=%fused_computation.194 | output fusion | flops 9437247 | bytes 12943360 | tf_op jit(solution)/shard_map/sub | solution.py:65
  224.1 8.9 %convert_bitcast_fusion.1 = bf16[24,64,16,32]{1,3,2,0:T(8,128)(2,1)} fusion(f32[24,16,64,64]{2,3,1,0:T(8,128)} %get-tuple-element.43, f32[24,16,64]{2,1,0:T(8,128)S(1)} %get-tuple-element.42, bf16[24,64,1,16,32]{1,4,3,0,2:T(8,128)(2,1)} %copy.170), kind=kOutput, calls=%fused_computation.101 | convolution fusion | flops 104595456 | bytes 9535488 | tf_op jit(solution)/shard_map/nhqk,nkhd->nqhd/dot_general | solution.py:68
  241.0 8.4 %reshape.257 = bf16[6,4,8,8,512]{4,3,2,1,0:T(8,128)(2,1)S(1)} reshape(bf16[24,64,16,32]{3,2,1,0:T(8,128)(2,1)} %copy.123) | data formatting | bytes 3145728 | tf_op jit(solution)/shard_map/reshape | solution.py:141
  257.6 13.2 %constant_dynamic-slice_fusion = (bf16[48,2,1,1,1536]{4,2,1,0,3:T(2,128)(2,1)S(1)}, bf16[48,2,1,1,1536]{4,2,1,0,3:T(2,128)(2,1)S(1)}, bf16[48,2,1,1,1536]{4,2,1,...) fusion(bf16[48,2,16,1,1536]{4,2,1,0,3:T(8,128)(2,1)S(1)} %bitca, ...), kind=kLoop, calls=%fused_computation.155 | loop fusion | bytes 9437248 | tf_op jit(solution)/shard_map/dynamic-slice.15
  294.0 11.7 %collective-permute-done.7 = bf16[48,2,1,1536]{3,0,1,2:T(8,128)(2,1)S(1)} collective-permute-done((bf16[48,2,1,1536]{3,0,1,2:T(8,128)(2,1)S(1)}, bf16[48,2,1,1536]{3,0,1,2:T(8,128)(2,1)S(1)}, u32[]{:S(2)}, u32[]{:S(2)}) %collective-permute-start.7) | collective-permute-done | bytes 294944 | tf_op jit(solution)/shard_map/ppermute | solution.py:179
  318.4 25.4 %collective-permute-done.10 = bf16[48,2,1,1536]{3,0,1,2:T(8,128)(2,1)S(1)} collective-permute-done((bf16[48,2,1,1536]{3,0,1,2:T(8,128)(2,1)S(1)}, bf16[48,2,1,1536]{3,0,1,2:T(8,128)(2,1)S(1)}, u32[]{:S(2)}, u32[]{:S(2)}) %collective-permute-start.10) | collective-permute-done | bytes 294944 | tf_op jit(solution)/shard_map/ppermute | solution.py:179
  349.8 18.9 %collective-permute-done.12 = bf16[48,2,1,1536]{3,0,1,2:T(8,128)(2,1)S(1)} collective-permute-done((bf16[48,2,1,1536]{3,0,1,2:T(8,128)(2,1)S(1)}, bf16[48,2,1,1536]{3,0,1,2:T(8,128)(2,1)S(1)}, u32[]{:S(2)}, u32[]{:S(2)}) %collective-permute-start.12) | collective-permute-done | bytes 294944 | tf_op jit(solution)/shard_map/ppermute | solution.py:179
  377.9 9.4 %copy.156 = bf16[48,2,16,1,1536]{4,1,2,0,3:T(2,128)(2,1)} copy(bf16[48,2,16,1,1536]{4,0,1,2,3:T(8,128)(2,1)} %bitcast.210) | data formatting | bytes 9437184 | tf_op jit(solution)/shard_map/transpose | solution.py:18
  392.9 21.1 %reshape_reshape.14 = bf16[24,64,3,16,32]{4,3,2,1,0:T(8,128)(2,1)} reshape(bf16[6,2,2,8,8,1536]{5,4,3,2,1,0:T(8,128)(2,1)} %copy.157) | data formatting | bytes 9437184 | tf_op jit(solution)/shard_map/reshape;reshape | solution.py:165
  414.0 14.3 %fusion.89 = (bf16[24,64,1,16,32]{4,3,2,1,0:T(8,128)(2,1)}, bf16[24,64,1,16,32]{4,3,2,1,0:T(8,128)(2,1)}, bf16[24,64,1,16,32]{4,3,2,1,0:T(8,128)(2,1)}) fusion(bf16[24,64,3,16,32]{4,3,2,1,0:T(8,128)(2,1)} %reshape_reshape.14), kind=kLoop, calls=%fused_computation.190 | loop fusion | bytes 9437184 | tf_op jit(solution)/shard_map/slice | solution.py:69
  428.3 8.2 %copy.190 = bf16[24,64,1,16,32]{1,4,3,0,2:T(8,128)(2,1)} copy(bf16[24,64,1,16,32]{4,3,2,1,0:T(8,128)(2,1)} %get-tuple-element.8) | data formatting | bytes 3145728
  444.5 8.1 %copy.189 = bf16[24,64,1,16,32]{1,4,3,0,2:T(8,128)(2,1)} copy(bf16[24,64,1,16,32]{4,3,2,1,0:T(8,128)(2,1)} %get-tuple-element.7) | data formatting | bytes 3145728
  457.3 8.1 %fusion.94 = (f32[24,16,64]{2,1,0:T(8,128)S(1)}, f32[24,16,64,64]{2,3,1,0:T(8,128)}) fusion(f32[24,16,64,64]{2,3,1,0:T(8,128)S(1)} %fusion.49, f32[16,64,64]{1,2,0:T(8,128)S(1)} %copy-done.3), kind=kOutput, calls=%fused_computation.195 | output fusion | flops 9437247 | bytes 12943360 | tf_op jit(solution)/shard_map/sub | solution.py:65
  465.4 8.9 %convert_bitcast_fusion = bf16[24,64,16,32]{1,3,2,0:T(8,128)(2,1)} fusion(f32[24,16,64,64]{2,3,1,0:T(8,128)} %get-tuple-element.47, f32[24,16,64]{2,1,0:T(8,128)S(1)} %get-tuple-element.46, bf16[24,64,1,16,32]{1,4,3,0,2:T(8,128)(2,1)} %copy.189), kind=kOutput, calls=%fused_computation.100 | convolution fusion | flops 104595456 | bytes 9535488 | tf_op jit(solution)/shard_map/nhqk,nkhd->nqhd/dot_general | solution.py:68
  474.4 8.0 %copy.163 = bf16[24,64,16,32]{3,2,1,0:T(8,128)(2,1)} copy(bf16[24,64,16,32]{1,3,2,0:T(8,128)(2,1)} %convert_bitcast_fusion) | data formatting | bytes 3145728 | tf_op jit(solution)/shard_map/convert_element_type | solution.py:70
  482.4 9.5 %reshape_reshape.15 = bf16[6,2,2,8,8,512]{5,4,3,2,1,0:T(8,128)(2,1)} reshape(bf16[24,64,16,32]{3,2,1,0:T(8,128)(2,1)} %copy.163) | data formatting | bytes 3145728 | tf_op jit(solution)/shard_map/reshape;reshape | solution.py:159
  495.0 61.2 %all_to_all.5 = bf16[48,2,16,512]{3,1,0,2:T(2,128)(2,1)S(1)} all-to-all(bf16[48,2,16,512]{3,1,0,2:T(2,128)(2,1)S(1)} %bitcast.213), channel_id=1, replica_groups=mesh['groups'=2,'lon'=16] {'lon'}, dimensions={2} | all-to-all | bytes 3145728 | tf_op jit(solution)/shard_map/all_to_all | solution.py:194
  (136 shorter events, 148.8 us)
Async XLA Ops:
  1.6 36.9 %copy-start.8 = (f32[9,2048]{1,0:T(8,128)S(1)}, f32[9,2048]{1,0:T(8,128)}, u32[]{:S(2)}) copy-start(f32[9,2048]{1,0:T(8,128)} %param.19) | copy-start | bytes 221188
  1.6 37.0 %copy-start.14 = (f32[225,16]{0,1:T(8,128)S(1)}, f32[225,16]{0,1:T(8,128)}, u32[]{:S(2)}) copy-start(f32[225,16]{0,1:T(8,128)} %param.27) | copy-start | bytes 43204
  1.6 40.5 %copy-start.15 = (f32[225,16]{0,1:T(8,128)S(1)}, f32[225,16]{0,1:T(8,128)}, u32[]{:S(2)}) copy-start(f32[225,16]{0,1:T(8,128)} %param.31) | copy-start | bytes 43204
  35.8 11.6 %collective-permute-start = (bf16[48,1,2048]{2,1,0:T(2,128)(2,1)S(1)}, bf16[48,1,2048]{2,1,0:T(2,128)(2,1)S(1)}, u32[]{:S(2)}, u32[]{:S(2)}) collective-permute-start(bf16[48,1,2048]{2,1,0:T(2,128)(2,1)S(1)} %get-tuple-element.13), channel_id=1, source_target_pairs={{0,1},{1,2},{2,3},{3,4},{4,5},{5,6},{6,7},{7,8},{8,9},{9,10},{10,1... | collective-permute-start | bytes 589832 | tf_op jit(solution)/shard_map/ppermute | solution.py:32
  38.4 11.4 %collective-permute-start.1 = (bf16[48,1,2048]{2,1,0:T(2,128)(2,1)S(1)}, bf16[48,1,2048]{2,1,0:T(2,128)(2,1)S(1)}, u32[]{:S(2)}, u32[]{:S(2)}) collective-permute-start(bf16[48,1,2048]{2,1,0:T(2,128)(2,1)S(1)} %get-tuple-element.14), channel_id=1, source_target_pairs={{1,0},{2,1},{3,2},{4,3},{5,4},{6,5},{7,6},{8,7},{9,8},{10,9},{11,1... | collective-permute-start | bytes 589832 | tf_op jit(solution)/shard_map/ppermute | solution.py:34
  56.3 78.0 %copy-start.6 = (bf16[2048,128]{1,0:T(8,128)(2,1)S(1)}, bf16[2048,128]{1,0:T(8,128)(2,1)}, u32[]{:S(2)}) copy-start(bf16[2048,128]{1,0:T(8,128)(2,1)} %param.21) | copy-start | bytes 1572868
  56.3 78.3 %copy-start.7 = (bf16[128,2048]{1,0:T(8,128)(2,1)S(1)}, bf16[128,2048]{1,0:T(8,128)(2,1)}, u32[]{:S(2)}) copy-start(bf16[128,2048]{1,0:T(8,128)(2,1)} %param.22) | copy-start | bytes 1572868
  271.0 8.7 %collective-permute-start.2 = (bf16[48,2,1,1536]{3,0,1,2:T(8,128)(2,1)S(1)}, bf16[48,2,1,1536]{3,0,1,2:T(8,128)(2,1)S(1)}, u32[]{:S(2)}, u32[]{:S(2)}) collective-permute-start(bf16[48,2,1,1536]{3,0,1,2:T(8,128)(2,1)S(1)} %bitcast.234), channel_id=1, source_target_pairs={{0,1},{1,0},{2,3},{3,2},{4,5},{5,4},{6,7},{7,6},{8,9},{9,8},{10,11... | collective-permute-start | bytes 884744 | tf_op jit(solution)/shard_map/ppermute | solution.py:179
  273.8 8.7 %collective-permute-start.3 = (bf16[48,2,1,1536]{3,0,1,2:T(8,128)(2,1)S(1)}, bf16[48,2,1,1536]{3,0,1,2:T(8,128)(2,1)S(1)}, u32[]{:S(2)}, u32[]{:S(2)}) collective-permute-start(bf16[48,2,1,1536]{3,0,1,2:T(8,128)(2,1)S(1)} %bitcast.233), channel_id=1, source_target_pairs={{0,2},{1,3},{2,0},{3,1},{4,6},{5,7},{6,4},{7,5},{8,10},{9,11},{10,... | collective-permute-start | bytes 884744 | tf_op jit(solution)/shard_map/ppermute | solution.py:179
  274.0 15.2 %collective-permute-start.4 = (bf16[48,2,1,1536]{3,0,1,2:T(8,128)(2,1)S(1)}, bf16[48,2,1,1536]{3,0,1,2:T(8,128)(2,1)S(1)}, u32[]{:S(2)}, u32[]{:S(2)}) collective-permute-start(bf16[48,2,1,1536]{3,0,1,2:T(8,128)(2,1)S(1)} %bitcast.232), channel_id=1, source_target_pairs={{0,3},{1,2},{2,1},{3,0},{4,7},{5,6},{6,5},{7,4},{8,11},{9,10},{10,... | collective-permute-start | bytes 884744 | tf_op jit(solution)/shard_map/ppermute | solution.py:179
  275.8 14.2 %collective-permute-start.5 = (bf16[48,2,1,1536]{3,0,1,2:T(8,128)(2,1)S(1)}, bf16[48,2,1,1536]{3,0,1,2:T(8,128)(2,1)S(1)}, u32[]{:S(2)}, u32[]{:S(2)}) collective-permute-start(bf16[48,2,1,1536]{3,0,1,2:T(8,128)(2,1)S(1)} %bitcast.231), channel_id=1, source_target_pairs={{0,4},{1,5},{2,6},{3,7},{4,0},{5,1},{6,2},{7,3},{8,12},{9,13},{10,... | collective-permute-start | bytes 884744 | tf_op jit(solution)/shard_map/ppermute | solution.py:179
  276.0 17.2 %collective-permute-start.6 = (bf16[48,2,1,1536]{3,0,1,2:T(8,128)(2,1)S(1)}, bf16[48,2,1,1536]{3,0,1,2:T(8,128)(2,1)S(1)}, u32[]{:S(2)}, u32[]{:S(2)}) collective-permute-start(bf16[48,2,1,1536]{3,0,1,2:T(8,128)(2,1)S(1)} %bitcast.230), channel_id=1, source_target_pairs={{0,5},{1,4},{2,7},{3,6},{4,1},{5,0},{6,3},{7,2},{8,13},{9,12},{10,... | collective-permute-start | bytes 884744 | tf_op jit(solution)/shard_map/ppermute | solution.py:179
  279.7 25.9 %collective-permute-start.7 = (bf16[48,2,1,1536]{3,0,1,2:T(8,128)(2,1)S(1)}, bf16[48,2,1,1536]{3,0,1,2:T(8,128)(2,1)S(1)}, u32[]{:S(2)}, u32[]{:S(2)}) collective-permute-start(bf16[48,2,1,1536]{3,0,1,2:T(8,128)(2,1)S(1)} %bitcast.229), channel_id=1, source_target_pairs={{0,6},{1,7},{2,4},{3,5},{4,2},{5,3},{6,0},{7,1},{8,14},{9,15},{10,... | collective-permute-start | bytes 884744 | tf_op jit(solution)/shard_map/ppermute | solution.py:179
  282.5 30.3 %collective-permute-start.8 = (bf16[48,2,1,1536]{3,0,1,2:T(8,128)(2,1)S(1)}, bf16[48,2,1,1536]{3,0,1,2:T(8,128)(2,1)S(1)}, u32[]{:S(2)}, u32[]{:S(2)}) collective-permute-start(bf16[48,2,1,1536]{3,0,1,2:T(8,128)(2,1)S(1)} %bitcast.228), channel_id=1, source_target_pairs={{0,7},{1,6},{2,5},{3,4},{4,3},{5,2},{6,1},{7,0},{8,15},{9,14},{10,... | collective-permute-start | bytes 884744 | tf_op jit(solution)/shard_map/ppermute | solution.py:179
  289.2 28.3 %collective-permute-start.9 = (bf16[48,2,1,1536]{3,0,1,2:T(8,128)(2,1)S(1)}, bf16[48,2,1,1536]{3,0,1,2:T(8,128)(2,1)S(1)}, u32[]{:S(2)}, u32[]{:S(2)}) collective-permute-start(bf16[48,2,1,1536]{3,0,1,2:T(8,128)(2,1)S(1)} %bitcast.227), channel_id=1, source_target_pairs={{0,8},{1,9},{2,10},{3,11},{4,12},{5,13},{6,14},{7,15},{8,0},{9,1},... | collective-permute-start | bytes 884744 | tf_op jit(solution)/shard_map/ppermute | solution.py:179
  290.0 53.8 %collective-permute-start.10 = (bf16[48,2,1,1536]{3,0,1,2:T(8,128)(2,1)S(1)}, bf16[48,2,1,1536]{3,0,1,2:T(8,128)(2,1)S(1)}, u32[]{:S(2)}, u32[]{:S(2)}) collective-permute-start(bf16[48,2,1,1536]{3,0,1,2:T(8,128)(2,1)S(1)} %bitcast.226), channel_id=1, source_target_pairs={{0,9},{1,8},{2,11},{3,10},{4,13},{5,12},{6,15},{7,14},{8,1},{9,0},... | collective-permute-start | bytes 884744 | tf_op jit(solution)/shard_map/ppermute | solution.py:179
  293.2 55.7 %collective-permute-start.11 = (bf16[48,2,1,1536]{3,0,1,2:T(8,128)(2,1)S(1)}, bf16[48,2,1,1536]{3,0,1,2:T(8,128)(2,1)S(1)}, u32[]{:S(2)}, u32[]{:S(2)}) collective-permute-start(bf16[48,2,1,1536]{3,0,1,2:T(8,128)(2,1)S(1)} %bitcast.225), channel_id=1, source_target_pairs={{0,10},{1,11},{2,8},{3,9},{4,14},{5,15},{6,12},{7,13},{8,2},{9,3},... | collective-permute-start | bytes 884744 | tf_op jit(solution)/shard_map/ppermute | solution.py:179
  305.6 63.1 %collective-permute-start.12 = (bf16[48,2,1,1536]{3,0,1,2:T(8,128)(2,1)S(1)}, bf16[48,2,1,1536]{3,0,1,2:T(8,128)(2,1)S(1)}, u32[]{:S(2)}, u32[]{:S(2)}) collective-permute-start(bf16[48,2,1,1536]{3,0,1,2:T(8,128)(2,1)S(1)} %bitcast.224), channel_id=1, source_target_pairs={{0,11},{1,10},{2,9},{3,8},{4,15},{5,14},{6,13},{7,12},{8,3},{9,2},... | collective-permute-start | bytes 884744 | tf_op jit(solution)/shard_map/ppermute | solution.py:179
  312.8 56.8 %collective-permute-start.13 = (bf16[48,2,1,1536]{3,0,1,2:T(8,128)(2,1)S(1)}, bf16[48,2,1,1536]{3,0,1,2:T(8,128)(2,1)S(1)}, u32[]{:S(2)}, u32[]{:S(2)}) collective-permute-start(bf16[48,2,1,1536]{3,0,1,2:T(8,128)(2,1)S(1)} %bitcast.223), channel_id=1, source_target_pairs={{0,12},{1,13},{2,14},{3,15},{4,8},{5,9},{6,10},{7,11},{8,4},{9,5},... | collective-permute-start | bytes 884744 | tf_op jit(solution)/shard_map/ppermute | solution.py:179
  317.6 52.8 %collective-permute-start.14 = (bf16[48,2,1,1536]{3,0,1,2:T(8,128)(2,1)S(1)}, bf16[48,2,1,1536]{3,0,1,2:T(8,128)(2,1)S(1)}, u32[]{:S(2)}, u32[]{:S(2)}) collective-permute-start(bf16[48,2,1,1536]{3,0,1,2:T(8,128)(2,1)S(1)} %bitcast.222), channel_id=1, source_target_pairs={{0,13},{1,12},{2,15},{3,14},{4,9},{5,8},{6,11},{7,10},{8,5},{9,4},... | collective-permute-start | bytes 884744 | tf_op jit(solution)/shard_map/ppermute | solution.py:179
  343.8 27.3 %collective-permute-start.15 = (bf16[48,2,1,1536]{3,0,1,2:T(8,128)(2,1)S(1)}, bf16[48,2,1,1536]{3,0,1,2:T(8,128)(2,1)S(1)}, u32[]{:S(2)}, u32[]{:S(2)}) collective-permute-start(bf16[48,2,1,1536]{3,0,1,2:T(8,128)(2,1)S(1)} %bitcast.221), channel_id=1, source_target_pairs={{0,14},{1,15},{2,12},{3,13},{4,10},{5,11},{6,8},{7,9},{8,6},{9,7},... | collective-permute-start | bytes 884744 | tf_op jit(solution)/shard_map/ppermute | solution.py:179
  348.9 23.0 %collective-permute-start.16 = (bf16[48,2,1,1536]{3,0,1,2:T(8,128)(2,1)S(1)}, bf16[48,2,1,1536]{3,0,1,2:T(8,128)(2,1)S(1)}, u32[]{:S(2)}, u32[]{:S(2)}) collective-permute-start(bf16[48,2,1,1536]{3,0,1,2:T(8,128)(2,1)S(1)} %bitcast.220), channel_id=1, source_target_pairs={{0,15},{1,14},{2,13},{3,12},{4,11},{5,10},{6,9},{7,8},{8,7},{9,6},... | collective-permute-start | bytes 884744 | tf_op jit(solution)/shard_map/ppermute | solution.py:179
  474.4 83.4 %copy-start.13 = (bf16[512,512]{1,0:T(8,128)(2,1)S(1)}, bf16[512,512]{1,0:T(8,128)(2,1)}, u32[]{:S(2)}) copy-start(bf16[512,512]{1,0:T(8,128)(2,1)} %param.30) | copy-start | bytes 1572868
  474.4 87.0 %copy-start.1 = (bf16[512,2048]{1,0:T(8,128)(2,1)S(1)}, bf16[512,2048]{1,0:T(8,128)(2,1)}, u32[]{:S(2)}) copy-start(bf16[512,2048]{1,0:T(8,128)(2,1)} %param.17) | copy-start | bytes 6291460
  (11 other events, 106.7 us)
